TPU v7x, 512 devices: a whole 4x4x16 slice. The times are simulated.
512 devices in a mesh: dp: 64 (over z, x_hi, core), coef: 8 (over y, x_lo).
Axes of the slice: x: 4 (x_hi: 2, x_lo: 2; x = x_hi * 2 + x_lo), y: 4, z: 16, core: 2. Of those that a mesh axis runs over, the one named last changes fastest.
Arguments:
- location: int32 [32768], P('dp'), may hold values from 0 to 1023
- component: int32 [32768], P('dp'), may hold values from 0 to 2
- epoch_bin: int32 [32768], P('dp'), may hold values from 0 to 127
- residual: bfloat16 [32768], P('dp'), may hold values from -6 to 6
- row_scale: bfloat16 [32768], P('dp'), may hold values from 0.5 to 2
- spatial_table: bfloat16 [3072, 3072], P(None, 'coef'), may hold values from -1 to 3
- spline_table: bfloat16 [128, 3072], P(None, 'coef'), may hold values from 0 to 1
Outputs:
- gram_band: float32 [8, 384, 1920], P('coef', 'dp')
- gradient: float32 [8, 384], P('coef', 'dp')
All inputs are finite; a program needn't handle non-finite values.
Results may differ from a plain program's by a relative error of at most 0.0042.
The roundings to bfloat16 on the way count: a program that leaves them out, or rounds other values in their place, can miss the bound.
Values may be sent and summed in bfloat16 or wider, within the bound.
A program may use at most 64 MiB of HBM per device.

v0:
```python
import math

import jax
import jax.numpy as jnp
from jax import lax
from jax.sharding import PartitionSpec as P


def from_behind(value, axis, steps):
    count = lax.axis_size(axis)
    pairs = [(source, (source + steps) % count) for source in range(count)]
    return lax.ppermute(value, axis, pairs)


def design_panel(spatial_index, spline_index, row_weight, tables, split_at):
    spatial_part = tables[:split_at]
    spline_part = tables[split_at:]
    spatial_value = jnp.take(spatial_part, spatial_index, axis=0).astype(jnp.float32)
    spline_value = jnp.take(spline_part, spline_index, axis=0).astype(jnp.float32)
    return (spatial_value * spline_value * row_weight[:, None]).astype(jnp.bfloat16)


def cross(left_panel, right_panel):
    return lax.dot_general(
        left_panel, right_panel, (((0,), (0,)), ((), ())), preferred_element_type=jnp.float32
    )


def local(location, component, epoch_bin, residual, row_scale, spatial_table, spline_table):
    spatial_count = spatial_table.shape[0]
    total_rows = location.shape[0] * lax.axis_size("dp")
    row_weight = row_scale.astype(jnp.float32) * (1.0 / math.sqrt(total_rows))
    spatial_index = 3 * location + component
    stacked = jnp.concatenate([spatial_table, spline_table], axis=0)
    own_panel = design_panel(spatial_index, epoch_bin, row_weight, stacked, spatial_count)
    whitened = (row_scale.astype(jnp.float32) * residual.astype(jnp.float32)).astype(jnp.bfloat16)
    self_tile = cross(own_panel, own_panel)
    gradient_part = cross(own_panel, whitened)
    band_rows, gradient_rows = (
        lax.psum_scatter(self_tile, "dp", scatter_dimension=0, tiled=True),
        lax.psum_scatter(gradient_part, "dp", scatter_dimension=0, tiled=True),
    )
    pieces = [band_rows]
    moving = stacked
    for offset in range(1, lax.axis_size("coef") // 2 + 1):
        moving = from_behind(moving, "coef", -1)
        partner = design_panel(spatial_index, epoch_bin, row_weight, moving, spatial_count)
        pieces.append(
            lax.psum_scatter(cross(own_panel, partner), "dp", scatter_dimension=0, tiled=True)
        )
    gram_band = jnp.concatenate(pieces, axis=1)
    return (gram_band[None], gradient_rows[None])


def solution(mesh):
    return jax.shard_map(
        local,
        mesh=mesh,
        in_specs=(P("dp"), P("dp"), P("dp"), P("dp"), P("dp"), P(None, "coef"), P(None, "coef")),
        out_specs=(P("coef", "dp", None), P("coef", "dp")),
        check_vma=False,
    )
```

profile of v0, /device:TPU:24, one launch (start us, length us, event | category | flops | bytes accessed | tf_op | source)
XLA Modules:
  0.0 805.0 jit_solution(12058726354575666690)
XLA Ops:
  7.2 0.0 all-reduce.9.cloned.1.call-start
  7.2 2.0 pad_maximum_fusion
  9.3 0.0 copy-start.1
  9.3 3.7 collective-permute-start
  13.0 53.4 %collective-permute-done = bf16[3200,384]{1,0:T(8,128)(2,1)S(1)} collective-permute-done((bf16[3200,384]{1,0:T(8,128)(2,1)S(1)}, bf16[3200,384]{1,0:T(8,128)(2,1)S(1)}, u32[]{:S(2)}, u32[]{:S(2)}) %collective-permute-start) | collective-permute-done | bytes 2457632 | tf_op jit(solution)/shard_map/ppermute | solution.py:12
  66.4 4.5 collective-permute-start.1
  70.9 52.1 %collective-permute-done.1 = bf16[3200,384]{1,0:T(8,128)(2,1)S(1)} collective-permute-done((bf16[3200,384]{1,0:T(8,128)(2,1)S(1)}, bf16[3200,384]{1,0:T(8,128)(2,1)S(1)}, u32[]{:S(2)}, u32[]{:S(2)}) %collective-permute-start.1) | collective-permute-done | bytes 2457632 | tf_op jit(solution)/shard_map/ppermute | solution.py:12
  123.0 1.5 copy-done.2
  124.4 4.9 collective-permute-start.2
  129.4 51.1 %collective-permute-done.2 = bf16[3200,384]{1,0:T(8,128)(2,1)} collective-permute-done((bf16[3200,384]{1,0:T(8,128)(2,1)S(1)}, bf16[3200,384]{1,0:T(8,128)(2,1)}, u32[]{:S(2)}, u32[]{:S(2)}) %collective-permute-start.2) | collective-permute-done | bytes 2457632 | tf_op jit(solution)/shard_map/ppermute | solution.py:12
  180.5 5.1 collective-permute-start.3
  185.7 1.9 gather_fusion.1
  187.7 1.9 gather_fusion
  189.7 0.3 multiply_convert_fusion.4
  190.0 1.2 fusion.33
  191.2 0.9 slice.53
  192.1 1.9 gather_fusion.3
  194.1 1.9 slice.52
  196.0 1.9 gather_fusion.2
  197.9 2.1 fusion
  200.0 0.9 slice.55
  200.9 1.9 gather_fusion.5
  202.9 1.9 slice.54
  204.8 1.9 gather_fusion.4
  206.7 2.1 fusion.1
  208.8 0.9 slice.57
  209.7 1.9 gather_fusion.7
  211.7 1.9 slice.56
  213.6 1.9 gather_fusion.6
  215.5 2.2 fusion.2
  217.7 18.3 %collective-permute-done.3 = bf16[3200,384]{1,0:T(8,128)(2,1)} collective-permute-done((bf16[3200,384]{1,0:T(8,128)(2,1)}, bf16[3200,384]{1,0:T(8,128)(2,1)}, u32[]{:S(2)}, u32[]{:S(2)}) %collective-permute-start.3) | collective-permute-done | bytes 2457632 | tf_op jit(solution)/shard_map/ppermute | solution.py:12
  236.0 1.9 slice.58
  237.9 1.9 gather_fusion.8
  239.9 0.9 slice.59
  240.8 1.9 gather_fusion.9
  242.7 1.4 fusion.3
  244.1 0.0 all-reduce.9.cloned.1.call-update
  244.2 1.3 dynamic-slice
  246.1 0.2 convolution_reduce_fusion
  246.3 140.9 %all-reduce.5 = f32[384]{0:T(512)S(1)} all-reduce(f32[384]{0:T(512)S(1)} %convolution_reduce_fusion), channel_id=7, replica_groups=mesh['dp'=64,'coef'=8] {'dp'}, use_global_device_ids=true, to_apply=%region_5.8.clone | all-reduce | flops 384 | bytes 3072
  387.2 0.6 dynamic-slice_bitcast_fusion
  387.8 405.9 %all-reduce.9.cloned.1.call-done = (f32[384,384]{1,0:T(8,128)}, f32[384,384]{1,0:T(8,128)}, f32[384,384]{1,0:T(8,128)}, f32[384,384]{1,0:T(8,128)}, f32[384,384]{1,0:T(8,128)}) async-done(((f32[384,384]{1,0:T(8,128)}, f32[384,384]{1,0:T(8,128)}, f32[384,384]{1,0:T(8,128)}, f32[384,384]{1,0:T(8,128)}, f32[384,384]{1,0:T(8,128)}), (f32[384,384]{1,0:T(8,128)}, f32[384,384]{1,0:T(8,128)}, f32[384,384]{1,0:T(8,128)}, ...) | async-done | bytes 2949136
  793.8 0.7 dynamic-slice_dynamic-update-slice_fusion.4
  794.5 0.7 dynamic-slice_dynamic-update-slice_fusion.3
  795.3 0.7 dynamic-slice_dynamic-update-slice_fusion.2
  796.0 0.7 dynamic-slice_dynamic-update-slice_fusion.1
  796.7 0.7 dynamic-slice_dynamic-update-slice_fusion
  797.5 0.7 copy.10
  (30 shorter events, 0.1 us)
Async XLA Ops:
  7.2 178.6 %copy-start = (bf16[128,384]{1,0:T(8,128)(2,1)S(1)}, bf16[128,384]{1,0:T(8,128)(2,1)}, u32[]{:S(2)}) copy-start(bf16[128,384]{1,0:T(8,128)(2,1)} %param.17) | copy-start | bytes 294916
  7.2 178.5 %copy-start.4 = (s32[512]{0:T(512)S(1)}, s32[512]{0:T(512)}, u32[]{:S(2)}) copy-start(s32[512]{0:T(512)} %param.13) | copy-start | bytes 6148
  7.2 178.5 %copy-start.9 = (s32[512]{0:T(512)S(1)}, s32[512]{0:T(512)}, u32[]{:S(2)}) copy-start(s32[512]{0:T(512)} %param.12) | copy-start | bytes 6148
  7.2 178.5 %copy-start.10 = (s32[512]{0:T(512)S(1)}, s32[512]{0:T(512)}, u32[]{:S(2)}) copy-start(s32[512]{0:T(512)} %param.11) | copy-start | bytes 6148
  7.2 786.6 %all-reduce.9.cloned.1.call-start = ((), (), s32[]{:S(2)}) async-start(), calls=%async_computation | async-start | bytes 5898240
  9.3 178.5 %copy-start.1 = (bf16[3072,384]{1,0:T(8,128)(2,1)S(1)}, bf16[3072,384]{1,0:T(8,128)(2,1)}, u32[]{:S(2)}) copy-start(bf16[3072,384]{1,0:T(8,128)(2,1)} %param.16) | copy-start | bytes 7077892
  9.3 57.1 %collective-permute-start = (bf16[3200,384]{1,0:T(8,128)(2,1)S(1)}, bf16[3200,384]{1,0:T(8,128)(2,1)S(1)}, u32[]{:S(2)}, u32[]{:S(2)}) collective-permute-start(bf16[3200,384]{1,0:T(8,128)(2,1)S(1)} %pad_maximum_fusion), channel_id=1, source_target_pairs={{0,7},{1,0},{2,1},{3,2},{4,3},{5,4},{6,5},{7,6},{8,15},{9,8},{10,9... | collective-permute-start | bytes 7372808 | tf_op jit(solution)/shard_map/ppermute | solution.py:12
  66.4 114.1 %copy-start.3 = (bf16[3200,384]{1,0:T(8,128)(2,1)}, bf16[3200,384]{1,0:T(8,128)(2,1)S(1)}, u32[]{:S(2)}) copy-start(bf16[3200,384]{1,0:T(8,128)(2,1)S(1)} %collective-permute-done) | copy-start | bytes 7372804
  66.4 56.6 %collective-permute-start.1 = (bf16[3200,384]{1,0:T(8,128)(2,1)S(1)}, bf16[3200,384]{1,0:T(8,128)(2,1)S(1)}, u32[]{:S(2)}, u32[]{:S(2)}) collective-permute-start(bf16[3200,384]{1,0:T(8,128)(2,1)S(1)} %collective-permute-done), channel_id=1, source_target_pairs={{0,7},{1,0},{2,1},{3,2},{4,3},{5,4},{6,5},{7,6},{8,15},{9,8},{10,9... | collective-permute-start | bytes 7372808 | tf_op jit(solution)/shard_map/ppermute | solution.py:12
  123.0 1.5 copy-start.2
  124.4 56.1 %collective-permute-start.2 = (bf16[3200,384]{1,0:T(8,128)(2,1)S(1)}, bf16[3200,384]{1,0:T(8,128)(2,1)}, u32[]{:S(2)}, u32[]{:S(2)}) collective-permute-start(bf16[3200,384]{1,0:T(8,128)(2,1)S(1)} %collective-permute-done.1), channel_id=1, source_target_pairs={{0,7},{1,0},{2,1},{3,2},{4,3},{5,4},{6,5},{7,6},{8,15},{9,8},{10,9... | collective-permute-start | bytes 7372808 | tf_op jit(solution)/shard_map/ppermute | solution.py:12
  180.5 55.5 %collective-permute-start.3 = (bf16[3200,384]{1,0:T(8,128)(2,1)}, bf16[3200,384]{1,0:T(8,128)(2,1)}, u32[]{:S(2)}, u32[]{:S(2)}) collective-permute-start(bf16[3200,384]{1,0:T(8,128)(2,1)} %collective-permute-done.2), channel_id=1, source_target_pairs={{0,7},{1,0},{2,1},{3,2},{4,3},{5,4},{6,5},{7,6},{8,15},{9,8},{10,9... | collective-permute-start | bytes 7372808 | tf_op jit(solution)/shard_map/ppermute | solution.py:12
  185.7 4.0 copy-start.7
  187.7 2.0 copy-start.11
  187.7 2.0 copy-start.12
  189.7 1.5 copy-start.5
  239.8 2.9 copy-start.6
  239.8 2.9 copy-start.8
Sparse Core Ops, SparseCore 0:
  244.3 549.4 all-reduce.8
where the time goes:
time: 806 us; the launch traced here: 805 us
  waiting for transfers between devices  581 us (72%)
  blocking collectives  141 us (17%)
  local copies, waits for them, and re-layouts  38.4 us (5%)
  starting transfers between devices  18.3 us (2%)
  between operations  15.1 us (2%)
  matrix products  9.16 us (1%)
    unnamed x2, waiting for transfers between devices  406 us
    ppermute x4, waiting for transfers between devices, from_behind(): return lax.ppermute(value, axis, pairs)  175 us
    unnamed x1, blocking collectives  141 us
    ppermute x4, starting transfers between devices, from_behind(): return lax.ppermute(value, axis, pairs)  18.2 us
  transfers between devices with their start and end apart: 5, of which 5 were waited for; matrix products, arithmetic and copies ran while one was open for 4% of the time, Pallas kernels for 0%

commit v1 on v0

v1 whole, which is shorter than its diff:
```python
import math

import jax
import jax.numpy as jnp
from jax import lax
from jax.sharding import PartitionSpec as P

GROUPS = ((0, 1, 2), (3, 4))


def from_ahead(value, steps):
    count = lax.axis_size("coef")
    pairs = [((target + steps) % count, target) for target in range(count)]
    return lax.ppermute(value, "coef", pairs)


def swap(value, bit):
    count = lax.axis_size("dp")
    return lax.ppermute(value, "dp", [(source, source ^ bit) for source in range(count)])


def picked(table, index):
    hot = (index[:, None] == lax.broadcasted_iota(jnp.int32, (1, table.shape[0]), 1))
    return lax.dot_general(
        hot.astype(jnp.bfloat16), table, (((1,), (0,)), ((), ())),
        preferred_element_type=jnp.float32,
    )


def cross(left_panel, right_panel):
    return lax.dot_general(
        left_panel, right_panel, (((0,), (0,)), ((), ())), preferred_element_type=jnp.float32
    )


def scattered(keep, give, travel):
    count = lax.axis_size("dp")
    bit = 1
    while True:
        sent = [g.astype(t) for g, t in zip(give, travel)]
        if len(sent) > 1:
            sent = lax.optimization_barrier(sent)
        total = [k + swap(g, bit).astype(jnp.float32) for k, g in zip(keep, sent)]
        bit *= 2
        if bit == count:
            return total
        half = total[0].shape[0] // 2
        keep, give = [t[:half] for t in total], [t[half:] for t in total]


def local(location, component, epoch_bin, residual, row_scale, spatial_table, spline_table):
    dp = lax.axis_size("dp")
    me = lax.axis_index("dp")
    total_rows = location.shape[0] * dp
    scale = row_scale.astype(jnp.float32)
    row_weight = scale * (1.0 / math.sqrt(total_rows))
    own = (
        picked(spatial_table, 3 * location + component)
        * picked(spline_table, epoch_bin)
        * row_weight[:, None]
    ).astype(jnp.bfloat16)
    whitened = (scale * residual.astype(jnp.float32)).astype(jnp.bfloat16)

    panels = [own] + [from_ahead(own, k) for k in range(1, lax.axis_size("coef") // 2 + 1)]

    size = own.shape[1]
    each = size // dp
    place = lax.broadcasted_iota(jnp.int32, (1, size), 1)
    block, inner = place // each, place % each
    mirrored = jnp.zeros_like(block)
    bits = dp.bit_length() - 1
    for b in range(bits):
        mirrored = mirrored | (((block >> b) & 1) << (bits - 1 - b))
    wanted = each * (me ^ mirrored) + inner
    order = (lax.broadcasted_iota(jnp.int32, (size, 1), 0) == wanted).astype(jnp.bfloat16)
    left = lax.dot_general(
        own, order, (((1,), (0,)), ((), ())), preferred_element_type=jnp.float32
    ).astype(jnp.bfloat16)
    kept, given = left[:, : size // 2], left[:, size // 2 :]

    pieces = []
    given_piece = None
    for group in GROUPS:
        parts = [panels[k] for k in group]
        travel = [jnp.bfloat16]
        if given_piece is not None:
            parts, _ = lax.optimization_barrier((parts, given_piece))
        right = jnp.concatenate(parts, axis=1)
        given_piece = cross(given, right).astype(jnp.bfloat16)
        keep, give = [cross(kept, right)], [given_piece]
        if not pieces:
            keep.append(cross(kept, whitened))
            give.append(cross(given, whitened))
            travel.append(jnp.float32)
        total = scattered(keep, give, travel)
        pieces.append(total[0])
        if len(total) > 1:
            gradient = total[1]
    gram_band = jnp.concatenate(pieces, axis=1)
    return (gram_band[None], gradient[None])


def solution(mesh):
    return jax.shard_map(
        local,
        mesh=mesh,
        in_specs=(P("dp"), P("dp"), P("dp"), P("dp"), P("dp"), P(None, "coef"), P(None, "coef")),
        out_specs=(P("coef", "dp", None), P("coef", "dp")),
        check_vma=False,
    )
```

time: 806 us -> 167 us (0.21)
  the two profiles are of different devices: /device:TPU:24 before, /device:TPU:26 now
where the time goes in v1:
time: 167 us; the launch traced here: 166 us
  starting transfers between devices  101 us (60%)
  waiting for transfers between devices  52.6 us (31%)
  matrix products  8 us (5%)
  other arithmetic  2.31 us (1%)
    ppermute x18, starting transfers between devices, swap(): lax.ppermute(value, 'dp', [(source, source ^ bit) for source in range(cou...  85.3 us
    ppermute x18, waiting for transfers between devices, swap(): lax.ppermute(value, 'dp', [(source, source ^ bit) for source in range(cou...  28 us
    ppermute x4, waiting for transfers between devices, from_ahead(): return lax.ppermute(value, 'coef', pairs)  24.6 us
    ppermute x4, starting transfers between devices, from_ahead(): return lax.ppermute(value, 'coef', pairs)  15.2 us
    dot_general x6, matrix products, cross(): lax.dot_general(left_panel, right_panel, (((0,), (0,)), ((), ())), prefer...  4.42 us
  transfers between devices with their start and end apart: 22, of which 10 were waited for; matrix products, arithmetic and copies ran while one was open for 3% of the time, Pallas kernels for 0%

profile of v1, /device:TPU:26, one launch (start us, length us, event | category | flops | bytes accessed | tf_op | source)
XLA Modules:
  0.0 165.7 jit_solution(10254680762277843410)
XLA Ops:
  0.6 0.9 fusion.20
  1.5 1.3 fusion.6
  2.8 0.7 multiply_add_fusion
  3.5 1.9 %fusion.4 = bf16[512,384]{0,1:T(8,128)(2,1)S(1)} fusion(f32[512,384]{0,1:T(8,128)S(1)} %fusion.6, bf16[3072,384]{1,0:T(8,128)(2,1)S(1)} %copy-done, s32[512]{0:T(512)S(1)} %multiply_add_fusion, f32[512]{0:T(512)S(1)} %get-tuple-element.33), kind=kOutput, calls=%fused_computation.8 | convolution fusion | flops 1210122240 | bytes 3543040 | tf_op jit(solution)/shard_map/dot_general | solution.py:24
  5.4 2.4 %collective-permute-start = (bf16[512,384]{0,1:T(8,128)(2,1)S(1)}, bf16[512,384]{0,1:T(8,128)(2,1)}, u32[]{:S(2)}, u32[]{:S(2)}) collective-permute-start(bf16[512,384]{0,1:T(8,128)(2,1)S(1)} %fusion.4), channel_id=1, source_target_pairs={{1,0},{2,1},{3,2},{4,3},{5,4},{6,5},{7,6},{0,7},{9,8},{10,9},{11,1... | collective-permute-start | bytes 1179656 | tf_op jit(solution)/shard_map/ppermute | solution.py:14
  7.8 2.7 %collective-permute-start.1 = (bf16[512,384]{0,1:T(8,128)(2,1)S(1)}, bf16[512,384]{0,1:T(8,128)(2,1)}, u32[]{:S(2)}, u32[]{:S(2)}) collective-permute-start(bf16[512,384]{0,1:T(8,128)(2,1)S(1)} %fusion.4), channel_id=1, source_target_pairs={{2,0},{3,1},{4,2},{5,3},{6,4},{7,5},{0,6},{1,7},{10,8},{11,9},{12,... | collective-permute-start | bytes 1179656 | tf_op jit(solution)/shard_map/ppermute | solution.py:14
  10.5 3.2 %collective-permute-start.13 = (bf16[512,384]{0,1:T(8,128)(2,1)S(1)}, bf16[512,384]{0,1:T(8,128)(2,1)S(1)}, u32[]{:S(2)}, u32[]{:S(2)}) collective-permute-start(bf16[512,384]{0,1:T(8,128)(2,1)S(1)} %fusion.4), channel_id=1, source_target_pairs={{3,0},{4,1},{5,2},{6,3},{7,4},{0,5},{1,6},{2,7},{11,8},{12,9},{13,... | collective-permute-start | bytes 1179656 | tf_op jit(solution)/shard_map/ppermute | solution.py:14
  13.7 6.9 %collective-permute-start.14 = (bf16[512,384]{0,1:T(8,128)(2,1)S(1)}, bf16[512,384]{0,1:T(8,128)(2,1)S(1)}, u32[]{:S(2)}, u32[]{:S(2)}) collective-permute-start(bf16[512,384]{0,1:T(8,128)(2,1)S(1)} %fusion.4), channel_id=1, source_target_pairs={{4,0},{5,1},{6,2},{7,3},{0,4},{1,5},{2,6},{3,7},{12,8},{13,9},{14,... | collective-permute-start | bytes 1179656 | tf_op jit(solution)/shard_map/ppermute | solution.py:14
  20.6 0.4 convolution_convert_fusion.1
  21.1 2.9 %collective-permute-done = bf16[512,384]{0,1:T(8,128)(2,1)} collective-permute-done((bf16[512,384]{0,1:T(8,128)(2,1)S(1)}, bf16[512,384]{0,1:T(8,128)(2,1)}, u32[]{:S(2)}, u32[]{:S(2)}) %collective-permute-start) | collective-permute-done | bytes 393248 | tf_op jit(solution)/shard_map/ppermute | solution.py:14
  24.0 21.7 %collective-permute-done.1 = bf16[512,384]{0,1:T(8,128)(2,1)} collective-permute-done((bf16[512,384]{0,1:T(8,128)(2,1)S(1)}, bf16[512,384]{0,1:T(8,128)(2,1)}, u32[]{:S(2)}, u32[]{:S(2)}) %collective-permute-start.1) | collective-permute-done | bytes 393248 | tf_op jit(solution)/shard_map/ppermute | solution.py:14
  45.6 1.7 %convolution_convert_fusion = bf16[192,1152]{1,0:T(8,128)(2,1)S(1)} fusion(bf16[512,384]{0,1:T(8,128)(2,1)} %collective-permute-done.1, bf16[512,384]{0,1:T(8,128)(2,1)} %collective-permute-done, bf16[512,384]{0,1:T(8,128)(2,1)S(1)} %fusion.4, bf16[512,384]{0,1:T(8,128)(2,1)S(1)} %convolution_convert_fusion.1), kind=kOutput, calls=%fused_computation.4 | convolution fusion | flops 230252544 | bytes 1818624 | tf_op jit(solution)/shard_map/dot_general | solution.py:31
  47.4 0.4 convolution_convert_fusion.2
  47.8 1.9 %collective-permute-start.15 = (bf16[192,768]{1,0:T(8,128)(2,1)S(1)}, bf16[192,768]{1,0:T(8,128)(2,1)S(1)}, u32[]{:S(2)}, u32[]{:S(2)}) collective-permute-start(bf16[192,768]{1,0:T(8,128)(2,1)S(1)} %convolution_convert_fusion.2), channel_id=1, source_target_pairs={{0,8},{8,0},{16,24},{24,16},{32,40},{40,32},{48,56},{56,48},{64,72... | collective-permute-start | bytes 884744 | tf_op jit(solution)/shard_map/ppermute | solution.py:19
  49.7 1.5 collective-permute-done.15
  51.3 0.4 convolution_add_fusion.1
  51.7 4.0 %collective-permute-start.16 = (bf16[96,768]{1,0:T(8,128)(2,1)S(1)}, bf16[96,768]{1,0:T(8,128)(2,1)S(1)}, u32[]{:S(2)}, u32[]{:S(2)}) collective-permute-start(bf16[96,768]{1,0:T(8,128)(2,1)S(1)} %slice.198), channel_id=1, source_target_pairs={{0,16},{8,24},{16,0},{24,8},{32,48},{40,56},{48,32},{56,40},{64,80... | collective-permute-start | bytes 442376 | tf_op jit(solution)/shard_map/ppermute | solution.py:19
  55.8 0.1 fusion.8
  55.9 1.9 %collective-permute-start.2 = (bf16[192,1152]{1,0:T(8,128)(2,1)S(1)}, bf16[192,1152]{1,0:T(8,128)(2,1)S(1)}, u32[]{:S(2)}, u32[]{:S(2)}) collective-permute-start(bf16[192,1152]{1,0:T(8,128)(2,1)S(1)} %convolution_convert_fusion), channel_id=1, source_target_pairs={{0,8},{8,0},{16,24},{24,16},{32,40},{40,32},{48,56},{56,48},{64,72... | collective-permute-start | bytes 1327112 | tf_op jit(solution)/shard_map/ppermute | solution.py:19
  57.8 2.4 %collective-permute-start.3 = (f32[192]{0:T(256)S(1)}, f32[192]{0:T(256)S(1)}, u32[]{:S(2)}, u32[]{:S(2)}) collective-permute-start(f32[192]{0:T(256)S(1)} %bitcast.14), channel_id=1, source_target_pairs={{0,8},{8,0},{16,24},{24,16},{32,40},{40,32},{48,56},{56,48},{64,72... | collective-permute-start | bytes 2312 | tf_op jit(solution)/shard_map/ppermute | solution.py:19
  60.3 0.8 collective-permute-done.16
  61.1 3.8 %collective-permute-start.17 = (bf16[48,768]{1,0:T(8,128)(2,1)S(1)}, bf16[48,768]{1,0:T(8,128)(2,1)S(1)}, u32[]{:S(2)}, u32[]{:S(2)}) collective-permute-start(bf16[48,768]{1,0:T(8,128)(2,1)S(1)} %slice.200), channel_id=1, source_target_pairs={{0,32},{8,40},{16,48},{24,56},{32,0},{40,8},{48,16},{56,24},{64,96... | collective-permute-start | bytes 221192 | tf_op jit(solution)/shard_map/ppermute | solution.py:19
  64.9 0.1 fusion.12
  65.0 0.1 slice.110
  65.1 2.2 %collective-permute-done.17 = bf16[48,768]{1,0:T(8,128)(2,1)S(1)} collective-permute-done((bf16[48,768]{1,0:T(8,128)(2,1)S(1)}, bf16[48,768]{1,0:T(8,128)(2,1)S(1)}, u32[]{:S(2)}, u32[]{:S(2)}) %collective-permute-start.17) | collective-permute-done | bytes 73760 | tf_op jit(solution)/shard_map/ppermute | solution.py:19
  67.3 5.2 %collective-permute-start.18 = (bf16[24,768]{1,0:T(8,128)(2,1)S(1)}, bf16[24,768]{1,0:T(8,128)(2,1)S(1)}, u32[]{:S(2)}, u32[]{:S(2)}) collective-permute-start(bf16[24,768]{1,0:T(8,128)(2,1)S(1)} %slice.202), channel_id=1, source_target_pairs={{0,64},{8,72},{16,80},{24,88},{32,96},{40,104},{48,112},{56,120},{... | collective-permute-start | bytes 110600 | tf_op jit(solution)/shard_map/ppermute | solution.py:19
  72.5 1.7 %convolution_add_fusion = f32[192,1152]{1,0:T(8,128)S(1)} fusion(bf16[192,1152]{1,0:T(8,128)(2,1)S(1)} %collective-permute-done.2, bf16[512,384]{0,1:T(8,128)(2,1)} %collective-permute-done.1, bf16[512,384]{0,1:T(8,128)(2,1)} %collective-permute-done, bf16[512,384]{0,1:T(8,128)(2,1)S(1)} %fusion.4, bf16[512,384]{0,1:T(8,128)(2,1)S(1)} %convolution_convert_fusion.1), kind=kOutput, calls=%fused_computation.3 | convolution fusion | flops 230473728 | bytes 2703360 | tf_op jit(solution)/shard_map/dot_general | solution.py:31
  74.2 4.0 %collective-permute-start.5 = (f32[96]{0:T(128)S(1)}, f32[96]{0:T(128)S(1)}, u32[]{:S(2)}, u32[]{:S(2)}) collective-permute-start(f32[96]{0:T(128)S(1)} %slice.110), channel_id=1, source_target_pairs={{0,16},{8,24},{16,0},{24,8},{32,48},{40,56},{48,32},{56,40},{64,80... | collective-permute-start | bytes 1160 | tf_op jit(solution)/shard_map/ppermute | solution.py:19
  78.3 3.3 %collective-permute-start.4 = (bf16[96,1152]{1,0:T(8,128)(2,1)S(1)}, bf16[96,1152]{1,0:T(8,128)(2,1)S(1)}, u32[]{:S(2)}, u32[]{:S(2)}) collective-permute-start(bf16[96,1152]{1,0:T(8,128)(2,1)S(1)} %slice.197), channel_id=1, source_target_pairs={{0,16},{8,24},{16,0},{24,8},{32,48},{40,56},{48,32},{56,40},{64,80... | collective-permute-start | bytes 663560 | tf_op jit(solution)/shard_map/ppermute | solution.py:19
  81.6 9.1 %collective-permute-start.19 = (bf16[12,768]{1,0:T(8,128)(2,1)S(1)}, bf16[12,768]{1,0:T(8,128)(2,1)S(1)}, u32[]{:S(2)}, u32[]{:S(2)}) collective-permute-start(bf16[12,768]{1,0:T(8,128)(2,1)S(1)} %slice.204), channel_id=1, source_target_pairs={{0,128},{8,136},{16,144},{24,152},{32,160},{40,168},{48,176},{56,1... | collective-permute-start | bytes 55304 | tf_op jit(solution)/shard_map/ppermute | solution.py:19
  90.8 0.1 slice.114
  90.8 1.7 %collective-permute-done.19 = bf16[12,768]{1,0:T(8,128)(2,1)S(1)} collective-permute-done((bf16[12,768]{1,0:T(8,128)(2,1)S(1)}, bf16[12,768]{1,0:T(8,128)(2,1)S(1)}, u32[]{:S(2)}, u32[]{:S(2)}) %collective-permute-start.19) | collective-permute-done | bytes 18464 | tf_op jit(solution)/shard_map/ppermute | solution.py:19
  92.6 12.7 %collective-permute-start.20 = (bf16[6,768]{1,0:T(8,128)(2,1)S(1)}, bf16[6,768]{1,0:T(8,128)(2,1)S(1)}, u32[]{:S(2)}, u32[]{:S(2)}) collective-permute-start(bf16[6,768]{1,0:T(8,128)(2,1)S(1)} %slice.206), channel_id=1, source_target_pairs={{0,256},{8,264},{16,272},{24,280},{32,288},{40,296},{48,304},{56,3... | collective-permute-start | bytes 27656 | tf_op jit(solution)/shard_map/ppermute | solution.py:19
  105.3 2.9 %collective-permute-start.7 = (f32[48]{0:T(128)S(1)}, f32[48]{0:T(128)S(1)}, u32[]{:S(2)}, u32[]{:S(2)}) collective-permute-start(f32[48]{0:T(128)S(1)} %slice.114), channel_id=1, source_target_pairs={{0,32},{8,40},{16,48},{24,56},{32,0},{40,8},{48,16},{56,24},{64,96... | collective-permute-start | bytes 584 | tf_op jit(solution)/shard_map/ppermute | solution.py:19
  108.3 2.9 %collective-permute-start.6 = (bf16[48,1152]{1,0:T(8,128)(2,1)S(1)}, bf16[48,1152]{1,0:T(8,128)(2,1)S(1)}, u32[]{:S(2)}, u32[]{:S(2)}) collective-permute-start(bf16[48,1152]{1,0:T(8,128)(2,1)S(1)} %slice.199), channel_id=1, source_target_pairs={{0,32},{8,40},{16,48},{24,56},{32,0},{40,8},{48,16},{56,24},{64,96... | collective-permute-start | bytes 331784 | tf_op jit(solution)/shard_map/ppermute | solution.py:19
  111.2 0.1 slice.118
  111.3 3.6 %collective-permute-done.6 = bf16[48,1152]{1,0:T(8,128)(2,1)S(1)} collective-permute-done((bf16[48,1152]{1,0:T(8,128)(2,1)S(1)}, bf16[48,1152]{1,0:T(8,128)(2,1)S(1)}, u32[]{:S(2)}, u32[]{:S(2)}) %collective-permute-start.6) | collective-permute-done | bytes 110624 | tf_op jit(solution)/shard_map/ppermute | solution.py:19
  115.0 3.4 %collective-permute-start.9 = (f32[24]{0:T(128)S(1)}, f32[24]{0:T(128)S(1)}, u32[]{:S(2)}, u32[]{:S(2)}) collective-permute-start(f32[24]{0:T(128)S(1)} %slice.118), channel_id=1, source_target_pairs={{0,64},{8,72},{16,80},{24,88},{32,96},{40,104},{48,112},{56,120},{... | collective-permute-start | bytes 296 | tf_op jit(solution)/shard_map/ppermute | solution.py:19
  118.3 3.4 %collective-permute-start.8 = (bf16[24,1152]{1,0:T(8,128)(2,1)S(1)}, bf16[24,1152]{1,0:T(8,128)(2,1)S(1)}, u32[]{:S(2)}, u32[]{:S(2)}) collective-permute-start(bf16[24,1152]{1,0:T(8,128)(2,1)S(1)} %slice.201), channel_id=1, source_target_pairs={{0,64},{8,72},{16,80},{24,88},{32,96},{40,104},{48,112},{56,120},{... | collective-permute-start | bytes 165896 | tf_op jit(solution)/shard_map/ppermute | solution.py:19
  121.8 4.1 %collective-permute-done.8 = bf16[24,1152]{1,0:T(8,128)(2,1)S(1)} collective-permute-done((bf16[24,1152]{1,0:T(8,128)(2,1)S(1)}, bf16[24,1152]{1,0:T(8,128)(2,1)S(1)}, u32[]{:S(2)}, u32[]{:S(2)}) %collective-permute-start.8) | collective-permute-done | bytes 55328 | tf_op jit(solution)/shard_map/ppermute | solution.py:19
  125.9 4.5 %collective-permute-start.11 = (f32[12]{0:T(128)S(1)}, f32[12]{0:T(128)S(1)}, u32[]{:S(2)}, u32[]{:S(2)}) collective-permute-start(f32[12]{0:T(128)S(1)} %slice.122), channel_id=1, source_target_pairs={{0,128},{8,136},{16,144},{24,152},{32,160},{40,168},{48,176},{56,1... | collective-permute-start | bytes 152 | tf_op jit(solution)/shard_map/ppermute | solution.py:19
  130.4 5.3 %collective-permute-start.10 = (bf16[12,1152]{1,0:T(8,128)(2,1)S(1)}, bf16[12,1152]{1,0:T(8,128)(2,1)S(1)}, u32[]{:S(2)}, u32[]{:S(2)}) collective-permute-start(bf16[12,1152]{1,0:T(8,128)(2,1)S(1)} %slice.203), channel_id=1, source_target_pairs={{0,128},{8,136},{16,144},{24,152},{32,160},{40,168},{48,176},{56,1... | collective-permute-start | bytes 82952 | tf_op jit(solution)/shard_map/ppermute | solution.py:19
  135.8 4.4 %collective-permute-done.10 = bf16[12,1152]{1,0:T(8,128)(2,1)S(1)} collective-permute-done((bf16[12,1152]{1,0:T(8,128)(2,1)S(1)}, bf16[12,1152]{1,0:T(8,128)(2,1)S(1)}, u32[]{:S(2)}, u32[]{:S(2)}) %collective-permute-start.10) | collective-permute-done | bytes 27680 | tf_op jit(solution)/shard_map/ppermute | solution.py:19
  140.2 10.5 %collective-permute-start.21 = (f32[6]{0:T(128)S(1)}, f32[6]{0:T(128)S(1)}, u32[]{:S(2)}, u32[]{:S(2)}) collective-permute-start(f32[6]{0:T(128)S(1)} %slice.126), channel_id=1, source_target_pairs={{0,256},{8,264},{16,272},{24,280},{32,288},{40,296},{48,304},{56,3... | collective-permute-start | bytes 80 | tf_op jit(solution)/shard_map/ppermute | solution.py:19
  150.7 4.1 %collective-permute-start.12 = (bf16[6,1152]{1,0:T(8,128)(2,1)S(1)}, bf16[6,1152]{1,0:T(8,128)(2,1)S(1)}, u32[]{:S(2)}, u32[]{:S(2)}) collective-permute-start(bf16[6,1152]{1,0:T(8,128)(2,1)S(1)} %slice.205), channel_id=1, source_target_pairs={{0,256},{8,264},{16,272},{24,280},{32,288},{40,296},{48,304},{56,3... | collective-permute-start | bytes 41480 | tf_op jit(solution)/shard_map/ppermute | solution.py:19
  154.8 0.5 add_bitcast_fusion
  155.3 9.7 %collective-permute-done.12 = bf16[6,1152]{1,0:T(8,128)(2,1)S(1)} collective-permute-done((bf16[6,1152]{1,0:T(8,128)(2,1)S(1)}, bf16[6,1152]{1,0:T(8,128)(2,1)S(1)}, u32[]{:S(2)}, u32[]{:S(2)}) %collective-permute-start.12) | collective-permute-done | bytes 13856 | tf_op jit(solution)/shard_map/ppermute | solution.py:19
  165.1 0.7 copy.9
  (46 shorter events, 0.6 us)
Async XLA Ops:
  0.6 2.9 %copy-start = (bf16[3072,384]{1,0:T(8,128)(2,1)S(1)}, bf16[3072,384]{1,0:T(8,128)(2,1)}, u32[]{:S(2)}) copy-start(bf16[3072,384]{1,0:T(8,128)(2,1)} %param.12) | copy-start | bytes 7077892
  5.4 18.6 %collective-permute-start = (bf16[512,384]{0,1:T(8,128)(2,1)S(1)}, bf16[512,384]{0,1:T(8,128)(2,1)}, u32[]{:S(2)}, u32[]{:S(2)}) collective-permute-start(bf16[512,384]{0,1:T(8,128)(2,1)S(1)} %fusion.4), channel_id=1, source_target_pairs={{1,0},{2,1},{3,2},{4,3},{5,4},{6,5},{7,6},{0,7},{9,8},{10,9},{11,1... | collective-permute-start | bytes 1179656 | tf_op jit(solution)/shard_map/ppermute | solution.py:14
  7.8 37.8 %collective-permute-start.1 = (bf16[512,384]{0,1:T(8,128)(2,1)S(1)}, bf16[512,384]{0,1:T(8,128)(2,1)}, u32[]{:S(2)}, u32[]{:S(2)}) collective-permute-start(bf16[512,384]{0,1:T(8,128)(2,1)S(1)} %fusion.4), channel_id=1, source_target_pairs={{2,0},{3,1},{4,2},{5,3},{6,4},{7,5},{0,6},{1,7},{10,8},{11,9},{12,... | collective-permute-start | bytes 1179656 | tf_op jit(solution)/shard_map/ppermute | solution.py:14
  10.5 36.8 %collective-permute-start.13 = (bf16[512,384]{0,1:T(8,128)(2,1)S(1)}, bf16[512,384]{0,1:T(8,128)(2,1)S(1)}, u32[]{:S(2)}, u32[]{:S(2)}) collective-permute-start(bf16[512,384]{0,1:T(8,128)(2,1)S(1)} %fusion.4), channel_id=1, source_target_pairs={{3,0},{4,1},{5,2},{6,3},{7,4},{0,5},{1,6},{2,7},{11,8},{12,9},{13,... | collective-permute-start | bytes 1179656 | tf_op jit(solution)/shard_map/ppermute | solution.py:14
  13.7 33.6 %collective-permute-start.14 = (bf16[512,384]{0,1:T(8,128)(2,1)S(1)}, bf16[512,384]{0,1:T(8,128)(2,1)S(1)}, u32[]{:S(2)}, u32[]{:S(2)}) collective-permute-start(bf16[512,384]{0,1:T(8,128)(2,1)S(1)} %fusion.4), channel_id=1, source_target_pairs={{4,0},{5,1},{6,2},{7,3},{0,4},{1,5},{2,6},{3,7},{12,8},{13,9},{14,... | collective-permute-start | bytes 1179656 | tf_op jit(solution)/shard_map/ppermute | solution.py:14
  47.8 3.5 %collective-permute-start.15 = (bf16[192,768]{1,0:T(8,128)(2,1)S(1)}, bf16[192,768]{1,0:T(8,128)(2,1)S(1)}, u32[]{:S(2)}, u32[]{:S(2)}) collective-permute-start(bf16[192,768]{1,0:T(8,128)(2,1)S(1)} %convolution_convert_fusion.2), channel_id=1, source_target_pairs={{0,8},{8,0},{16,24},{24,16},{32,40},{40,32},{48,56},{56,48},{64,72... | collective-permute-start | bytes 884744 | tf_op jit(solution)/shard_map/ppermute | solution.py:19
  51.7 9.3 %collective-permute-start.16 = (bf16[96,768]{1,0:T(8,128)(2,1)S(1)}, bf16[96,768]{1,0:T(8,128)(2,1)S(1)}, u32[]{:S(2)}, u32[]{:S(2)}) collective-permute-start(bf16[96,768]{1,0:T(8,128)(2,1)S(1)} %slice.198), channel_id=1, source_target_pairs={{0,16},{8,24},{16,0},{24,8},{32,48},{40,56},{48,32},{56,40},{64,80... | collective-permute-start | bytes 442376 | tf_op jit(solution)/shard_map/ppermute | solution.py:19
  55.9 16.6 %collective-permute-start.2 = (bf16[192,1152]{1,0:T(8,128)(2,1)S(1)}, bf16[192,1152]{1,0:T(8,128)(2,1)S(1)}, u32[]{:S(2)}, u32[]{:S(2)}) collective-permute-start(bf16[192,1152]{1,0:T(8,128)(2,1)S(1)} %convolution_convert_fusion), channel_id=1, source_target_pairs={{0,8},{8,0},{16,24},{24,16},{32,40},{40,32},{48,56},{56,48},{64,72... | collective-permute-start | bytes 1327112 | tf_op jit(solution)/shard_map/ppermute | solution.py:19
  57.8 7.2 %collective-permute-start.3 = (f32[192]{0:T(256)S(1)}, f32[192]{0:T(256)S(1)}, u32[]{:S(2)}, u32[]{:S(2)}) collective-permute-start(f32[192]{0:T(256)S(1)} %bitcast.14), channel_id=1, source_target_pairs={{0,8},{8,0},{16,24},{24,16},{32,40},{40,32},{48,56},{56,48},{64,72... | collective-permute-start | bytes 2312 | tf_op jit(solution)/shard_map/ppermute | solution.py:19
  61.1 6.2 %collective-permute-start.17 = (bf16[48,768]{1,0:T(8,128)(2,1)S(1)}, bf16[48,768]{1,0:T(8,128)(2,1)S(1)}, u32[]{:S(2)}, u32[]{:S(2)}) collective-permute-start(bf16[48,768]{1,0:T(8,128)(2,1)S(1)} %slice.200), channel_id=1, source_target_pairs={{0,32},{8,40},{16,48},{24,56},{32,0},{40,8},{48,16},{56,24},{64,96... | collective-permute-start | bytes 221192 | tf_op jit(solution)/shard_map/ppermute | solution.py:19
  67.3 14.3 %collective-permute-start.18 = (bf16[24,768]{1,0:T(8,128)(2,1)S(1)}, bf16[24,768]{1,0:T(8,128)(2,1)S(1)}, u32[]{:S(2)}, u32[]{:S(2)}) collective-permute-start(bf16[24,768]{1,0:T(8,128)(2,1)S(1)} %slice.202), channel_id=1, source_target_pairs={{0,64},{8,72},{16,80},{24,88},{32,96},{40,104},{48,112},{56,120},{... | collective-permute-start | bytes 110600 | tf_op jit(solution)/shard_map/ppermute | solution.py:19
  74.2 16.5 %collective-permute-start.5 = (f32[96]{0:T(128)S(1)}, f32[96]{0:T(128)S(1)}, u32[]{:S(2)}, u32[]{:S(2)}) collective-permute-start(f32[96]{0:T(128)S(1)} %slice.110), channel_id=1, source_target_pairs={{0,16},{8,24},{16,0},{24,8},{32,48},{40,56},{48,32},{56,40},{64,80... | collective-permute-start | bytes 1160 | tf_op jit(solution)/shard_map/ppermute | solution.py:19
  78.3 26.9 %collective-permute-start.4 = (bf16[96,1152]{1,0:T(8,128)(2,1)S(1)}, bf16[96,1152]{1,0:T(8,128)(2,1)S(1)}, u32[]{:S(2)}, u32[]{:S(2)}) collective-permute-start(bf16[96,1152]{1,0:T(8,128)(2,1)S(1)} %slice.197), channel_id=1, source_target_pairs={{0,16},{8,24},{16,0},{24,8},{32,48},{40,56},{48,32},{56,40},{64,80... | collective-permute-start | bytes 663560 | tf_op jit(solution)/shard_map/ppermute | solution.py:19
  81.6 10.9 %collective-permute-start.19 = (bf16[12,768]{1,0:T(8,128)(2,1)S(1)}, bf16[12,768]{1,0:T(8,128)(2,1)S(1)}, u32[]{:S(2)}, u32[]{:S(2)}) collective-permute-start(bf16[12,768]{1,0:T(8,128)(2,1)S(1)} %slice.204), channel_id=1, source_target_pairs={{0,128},{8,136},{16,144},{24,152},{32,160},{40,168},{48,176},{56,1... | collective-permute-start | bytes 55304 | tf_op jit(solution)/shard_map/ppermute | solution.py:19
  92.6 15.7 %collective-permute-start.20 = (bf16[6,768]{1,0:T(8,128)(2,1)S(1)}, bf16[6,768]{1,0:T(8,128)(2,1)S(1)}, u32[]{:S(2)}, u32[]{:S(2)}) collective-permute-start(bf16[6,768]{1,0:T(8,128)(2,1)S(1)} %slice.206), channel_id=1, source_target_pairs={{0,256},{8,264},{16,272},{24,280},{32,288},{40,296},{48,304},{56,3... | collective-permute-start | bytes 27656 | tf_op jit(solution)/shard_map/ppermute | solution.py:19
  105.3 5.9 %collective-permute-start.7 = (f32[48]{0:T(128)S(1)}, f32[48]{0:T(128)S(1)}, u32[]{:S(2)}, u32[]{:S(2)}) collective-permute-start(f32[48]{0:T(128)S(1)} %slice.114), channel_id=1, source_target_pairs={{0,32},{8,40},{16,48},{24,56},{32,0},{40,8},{48,16},{56,24},{64,96... | collective-permute-start | bytes 584 | tf_op jit(solution)/shard_map/ppermute | solution.py:19
  108.3 6.6 %collective-permute-start.6 = (bf16[48,1152]{1,0:T(8,128)(2,1)S(1)}, bf16[48,1152]{1,0:T(8,128)(2,1)S(1)}, u32[]{:S(2)}, u32[]{:S(2)}) collective-permute-start(bf16[48,1152]{1,0:T(8,128)(2,1)S(1)} %slice.199), channel_id=1, source_target_pairs={{0,32},{8,40},{16,48},{24,56},{32,0},{40,8},{48,16},{56,24},{64,96... | collective-permute-start | bytes 331784 | tf_op jit(solution)/shard_map/ppermute | solution.py:19
  115.0 6.8 %collective-permute-start.9 = (f32[24]{0:T(128)S(1)}, f32[24]{0:T(128)S(1)}, u32[]{:S(2)}, u32[]{:S(2)}) collective-permute-start(f32[24]{0:T(128)S(1)} %slice.118), channel_id=1, source_target_pairs={{0,64},{8,72},{16,80},{24,88},{32,96},{40,104},{48,112},{56,120},{... | collective-permute-start | bytes 296 | tf_op jit(solution)/shard_map/ppermute | solution.py:19
  118.3 7.5 %collective-permute-start.8 = (bf16[24,1152]{1,0:T(8,128)(2,1)S(1)}, bf16[24,1152]{1,0:T(8,128)(2,1)S(1)}, u32[]{:S(2)}, u32[]{:S(2)}) collective-permute-start(bf16[24,1152]{1,0:T(8,128)(2,1)S(1)} %slice.201), channel_id=1, source_target_pairs={{0,64},{8,72},{16,80},{24,88},{32,96},{40,104},{48,112},{56,120},{... | collective-permute-start | bytes 165896 | tf_op jit(solution)/shard_map/ppermute | solution.py:19
  125.9 9.8 %collective-permute-start.11 = (f32[12]{0:T(128)S(1)}, f32[12]{0:T(128)S(1)}, u32[]{:S(2)}, u32[]{:S(2)}) collective-permute-start(f32[12]{0:T(128)S(1)} %slice.122), channel_id=1, source_target_pairs={{0,128},{8,136},{16,144},{24,152},{32,160},{40,168},{48,176},{56,1... | collective-permute-start | bytes 152 | tf_op jit(solution)/shard_map/ppermute | solution.py:19
  130.4 9.8 %collective-permute-start.10 = (bf16[12,1152]{1,0:T(8,128)(2,1)S(1)}, bf16[12,1152]{1,0:T(8,128)(2,1)S(1)}, u32[]{:S(2)}, u32[]{:S(2)}) collective-permute-start(bf16[12,1152]{1,0:T(8,128)(2,1)S(1)} %slice.203), channel_id=1, source_target_pairs={{0,128},{8,136},{16,144},{24,152},{32,160},{40,168},{48,176},{56,1... | collective-permute-start | bytes 82952 | tf_op jit(solution)/shard_map/ppermute | solution.py:19
  140.2 14.6 %collective-permute-start.21 = (f32[6]{0:T(128)S(1)}, f32[6]{0:T(128)S(1)}, u32[]{:S(2)}, u32[]{:S(2)}) collective-permute-start(f32[6]{0:T(128)S(1)} %slice.126), channel_id=1, source_target_pairs={{0,256},{8,264},{16,272},{24,280},{32,288},{40,296},{48,304},{56,3... | collective-permute-start | bytes 80 | tf_op jit(solution)/shard_map/ppermute | solution.py:19
  150.7 14.4 %collective-permute-start.12 = (bf16[6,1152]{1,0:T(8,128)(2,1)S(1)}, bf16[6,1152]{1,0:T(8,128)(2,1)S(1)}, u32[]{:S(2)}, u32[]{:S(2)}) collective-permute-start(bf16[6,1152]{1,0:T(8,128)(2,1)S(1)} %slice.205), channel_id=1, source_target_pairs={{0,256},{8,264},{16,272},{24,280},{32,288},{40,296},{48,304},{56,3... | collective-permute-start | bytes 41480 | tf_op jit(solution)/shard_map/ppermute | solution.py:19

commit v2 on v0

v2 whole, which is shorter than its diff:
```python
import functools
import math

import jax
import jax.numpy as jnp
from jax import lax
from jax.experimental import pallas as pl
from jax.experimental.pallas import tpu as pltpu
from jax.sharding import PartitionSpec as P

ORDERS = (((1, 2), (2, 2), (4, 4), (16, 4)), ((1, 2), (4, 4), (16, 4), (2, 2)))
GROUPS = ((0, 1, 2), (3, 4))
LANES = 128
MESH = pl.DeviceIdType.MESH


def picked(table, index):
    hot = (index[:, None] == lax.broadcasted_iota(jnp.int32, (1, table.shape[0]), 1))
    return lax.dot_general(
        hot.astype(jnp.bfloat16), table, (((1,), (0,)), ((), ())),
        preferred_element_type=jnp.float32,
    )


def partner(me, unit, choice):
    low = lax.rem(me // unit, 2)
    high = lax.rem(me // (2 * unit), 2)
    return me + (choice % 2) * unit * (1 - 2 * low) + (choice // 2) * 2 * unit * (1 - 2 * high)


def ordered(own, me, order):
    size = own.shape[1]
    blocks = math.prod(radix for _, radix in order)
    each = size // blocks
    place = lax.broadcasted_iota(jnp.int32, (1, size), 1)
    rest, inner = place // each, place % each
    mask = jnp.zeros_like(rest)
    for unit, radix in reversed(order):
        mask = mask + unit * (rest % radix)
        rest = rest // radix
    wanted = each * (me ^ mask) + inner
    hot = (lax.broadcasted_iota(jnp.int32, (size, 1), 0) == wanted).astype(jnp.bfloat16)
    return lax.dot_general(
        hot, own, (((0,), (1,)), ((), ())), preferred_element_type=jnp.float32
    ).astype(jnp.bfloat16)


def band_kernel(dp, coef, own_ref, left_a, left_b, slope_ref, band_ref, gradient_ref, *scratch):
    panels, send_a, send_b = scratch[0], scratch[1:5], scratch[5:9]
    recv_a, recv_b = scratch[9:13], scratch[13:17]
    panel_send, panel_recv, sum_send, sum_recv = scratch[17:21]
    me, mine = lax.axis_index("dp"), lax.axis_index("coef")
    pan = own_ref.shape[1]

    barrier = pltpu.get_barrier_semaphore()
    friends = [(me, lax.rem(mine + k, coef)) for k in range(1, coef)]
    friends += [(partner(me, u, q), mine) for u, r in ORDERS[0] for q in range(1, r)]
    for friend in friends:
        pl.semaphore_signal(barrier, inc=1, device_id=friend, device_id_type=MESH)
    pl.semaphore_wait(barrier, len(friends))

    fetches = []
    for k in range(1, coef // 2 + 1):
        fetch = pltpu.make_async_remote_copy(
            src_ref=own_ref,
            dst_ref=panels.at[k - 1],
            send_sem=panel_send.at[k - 1],
            recv_sem=panel_recv.at[k - 1],
            device_id=(me, lax.rem(mine + coef - k, coef)),
            device_id_type=MESH,
        )
        fetch.start()
        fetches.append(fetch)

    def packed(gram, slope):
        high = slope.astype(jnp.bfloat16).astype(jnp.float32)
        rest = slope - high
        middle = rest.astype(jnp.bfloat16).astype(jnp.float32)
        lane = lax.broadcasted_iota(jnp.int32, slope.shape, 1)
        three = jnp.where(lane == 0, high, jnp.where(lane == 1, middle, rest - middle))
        three = jnp.where(lane < 3, three, 0.0)
        return gram.astype(jnp.bfloat16), three.astype(jnp.bfloat16)

    def start(group, stage, values):
        unit, radix = ORDERS[group][stage]
        send, recv = (send_a, send_b)[group][stage], (recv_a, recv_b)[group][stage]
        chunk = values[0].shape[0] // radix
        copies = []
        for q in range(1, radix):
            cut = [v[q * chunk : (q + 1) * chunk] for v in values]
            if len(cut) == 2:
                gram, three = packed(*cut)
                width = gram.shape[1]
                send[q - 1, :, :width] = gram
                send[q - 1, :, width:] = three
            else:
                send[q - 1] = cut[0].astype(jnp.bfloat16)
            copy = pltpu.make_async_remote_copy(
                src_ref=send.at[q - 1],
                dst_ref=recv.at[q - 1],
                send_sem=sum_send.at[group, stage, q - 1],
                recv_sem=sum_recv.at[group, stage, q - 1],
                device_id=(partner(me, unit, q), mine),
                device_id_type=MESH,
            )
            copy.start()
            copies.append(copy)
        return copies, [v[:chunk] for v in values], recv

    def finish(state):
        copies, values, recv = state
        for q, copy in enumerate(copies):
            copy.wait()
            got = recv[q].astype(jnp.float32)
            width = values[0].shape[1]
            values = [values[0] + got[:, :width]] + [
                v + jnp.sum(got[:, width:], axis=1, keepdims=True) for v in values[1:]
            ]
        return values

    def product(left, k):
        right = own_ref[...] if k == 0 else panels[k - 1]
        return jnp.dot(left[...], right, preferred_element_type=jnp.float32)

    blocks = [product(left_a, 0)]
    for k in GROUPS[0][1:]:
        fetches[k - 1].wait()
        blocks.append(product(left_a, k))
    state_a = start(0, 0, [jnp.concatenate(blocks, axis=1), slope_ref[...]])
    blocks = []
    for k in GROUPS[1]:
        fetches[k - 1].wait()
        blocks.append(product(left_b, k))
    state_b = start(1, 0, [jnp.concatenate(blocks, axis=1)])
    for stage in range(1, len(ORDERS[0])):
        state_a = start(0, stage, finish(state_a))
        state_b = start(1, stage, finish(state_b))
    gram, slope = finish(state_a)
    band_ref[:, : gram.shape[1]] = gram
    gradient_ref[...] = slope
    band_ref[:, gram.shape[1] :] = finish(state_b)[0]


def band(own, left_a, left_b, slope):
    dp, coef = lax.axis_size("dp"), lax.axis_size("coef")
    rows, pan = own.shape
    widths = [len(GROUPS[0]) * pan + LANES, len(GROUPS[1]) * pan]
    buffers = []
    for order, width in zip(ORDERS, widths):
        left = pan
        for _, radix in order:
            left //= radix
            buffers.append(pltpu.VMEM((radix - 1, left, width), jnp.bfloat16))
    each = pan // dp
    vmem = pl.BlockSpec(memory_space=pltpu.VMEM)
    return pl.pallas_call(
        functools.partial(band_kernel, dp, coef),
        out_shape=(
            jax.ShapeDtypeStruct((each, (coef // 2 + 1) * pan), jnp.float32),
            jax.ShapeDtypeStruct((each, LANES), jnp.float32),
        ),
        in_specs=[vmem] * 4,
        out_specs=(vmem, vmem),
        scratch_shapes=[pltpu.VMEM((coef // 2, rows, pan), jnp.bfloat16)]
        + buffers
        + buffers
        + [
            pltpu.SemaphoreType.DMA((coef // 2,)),
            pltpu.SemaphoreType.DMA((coef // 2,)),
            pltpu.SemaphoreType.DMA((2, 4, 3)),
            pltpu.SemaphoreType.DMA((2, 4, 3)),
        ],
        compiler_params=pltpu.CompilerParams(
            collective_id=0, has_side_effects=True, vmem_limit_bytes=48 * 1024 * 1024
        ),
    )(own, left_a, left_b, slope)


def local(location, component, epoch_bin, residual, row_scale, spatial_table, spline_table):
    dp = lax.axis_size("dp")
    me = lax.axis_index("dp")
    total_rows = location.shape[0] * dp
    scale = row_scale.astype(jnp.float32)
    row_weight = scale * (1.0 / math.sqrt(total_rows))
    own = (
        picked(spatial_table, 3 * location + component)
        * picked(spline_table, epoch_bin)
        * row_weight[:, None]
    ).astype(jnp.bfloat16)
    whitened = (scale * residual.astype(jnp.float32)).astype(jnp.bfloat16)

    left_a, left_b = (ordered(own, me, order) for order in ORDERS)
    slope = lax.dot_general(
        left_a, whitened, (((1,), (0,)), ((), ())), preferred_element_type=jnp.float32
    )
    slope = jnp.broadcast_to(slope[:, None], (slope.shape[0], LANES))
    gram_band, gradient = band(own, left_a, left_b, slope)
    return (gram_band[None], gradient[None, :, 0])


def solution(mesh):
    return jax.shard_map(
        local,
        mesh=mesh,
        in_specs=(P("dp"), P("dp"), P("dp"), P("dp"), P("dp"), P(None, "coef"), P(None, "coef")),
        out_specs=(P("coef", "dp", None), P("coef", "dp")),
        check_vma=False,
    )
```

time: 806 us -> 85.8 us (0.11)
  the two profiles are of different devices: /device:TPU:24 before, /device:TPU:74 now
where the time goes in v2:
time: 85.8 us; the launch traced here: 85.6 us
  Pallas kernels  77.7 us (91%)
  matrix products  4.15 us (5%)
  other arithmetic  1.6 us (2%)
  local copies, waits for them, and re-layouts  1.42 us (2%)
    pallas_call x1, Pallas kernels, band(): pl.pallas_call(functools.partial(band_kernel, dp, coef), out_shape=(jax.S...  77.7 us
    dot_general x2, matrix products, picked(): lax.dot_general(hot.astype(jnp.bfloat16), table, (((1,), (0,)), ((), ()))...  3.06 us

profile of v2, /device:TPU:74, one launch (start us, length us, event | category | flops | bytes accessed | tf_op | source)
XLA Modules:
  0.0 85.6 jit_solution(2428312888816231239)
XLA Ops:
  0.6 0.0 copy-start
  0.6 0.9 multiply_add_fusion
  1.5 0.7 fusion.17
  2.3 1.2 %fusion.11 = f32[512,384]{1,0:T(8,128)S(1)} fusion(bf16[128,384]{1,0:T(8,128)(2,1)} %param.13, s32[512]{0:T(512)} %param.9), kind=kOutput, calls=%fused_computation.16 | convolution fusion | flops 50397184 | bytes 886784 | tf_op jit(solution)/shard_map/dot_general | solution.py:19
  3.5 0.0 copy-done
  3.5 1.8 %fusion.4.own_ref = bf16[512,384]{1,0:T(8,128)(2,1)S(1)} fusion(f32[512,384]{1,0:T(8,128)S(1)} %fusion.11, bf16[3072,384]{1,0:T(8,128)(2,1)S(1)} %copy-done, s32[512]{0:T(512)S(1)} %multiply_add_fusion, f32[512]{0:T(512)S(1)} %get-tuple-element.11), kind=kOutput, calls=%fused_computation.5 | convolution fusion | flops 1210122240 | bytes 3543040 | tf_op jit(solution)/shard_map/dot_general | solution.py:19
  5.3 0.4 convolution_convert_fusion.1.left_a
  5.8 0.3 convolution_reduce_fusion
  6.0 0.1 broadcast_in_dim.4.slope_ref
  6.1 0.4 convolution_convert_fusion.left_b
  6.6 77.7 %shard_map.86 = (f32[6,1920]{1,0:T(8,128)S(1)}, f32[6,128]{1,0:T(8,128)S(1)}) custom-call(bf16[512,384]{1,0:T(8,128)(2,1)S(1)} %fusion.4.own_ref, bf16[384,512]{1,0:T(8,128)(2,1)S(1)} %convolution_convert_fusion.1.left_a, bf16[384,512]{1,0:T(8,128)(2,1)S(1)} %convolution_convert_fusion.left_b, f32[384,128]{1,0:T(8,128)S(1)} %broadcast_in_dim.4.slope_ref), custom_call_target="tpu_custom_call" | custom-call | tf_op jit(solution)/shard_map/pallas_call | solution.py:156
  84.3 0.7 copy.10
  85.0 0.6 slice_reduce_fusion
  (2 shorter events, 0.1 us)
Async XLA Ops:
  0.6 2.9 %copy-start = (bf16[3072,384]{1,0:T(8,128)(2,1)S(1)}, bf16[3072,384]{1,0:T(8,128)(2,1)}, u32[]{:S(2)}) copy-start(bf16[3072,384]{1,0:T(8,128)(2,1)} %param.12) | copy-start | bytes 7077892

commit v3 on v2

--- a/solution.py
+++ b/solution.py
@@ -9,7 +9,7 @@
 from jax.sharding import PartitionSpec as P
 
 ORDERS = (((1, 2), (2, 2), (4, 4), (16, 4)), ((1, 2), (4, 4), (16, 4), (2, 2)))
-GROUPS = ((0, 1, 2), (3, 4))
+WAY = (0, 1, 0, 1, 0)
 LANES = 128
 MESH = pl.DeviceIdType.MESH
 
@@ -46,9 +46,11 @@
 
 
 def band_kernel(dp, coef, own_ref, left_a, left_b, slope_ref, band_ref, gradient_ref, *scratch):
-    panels, send_a, send_b = scratch[0], scratch[1:5], scratch[5:9]
-    recv_a, recv_b = scratch[9:13], scratch[13:17]
-    panel_send, panel_recv, sum_send, sum_recv = scratch[17:21]
+    panels = scratch[0]
+    stages, count = len(ORDERS[0]), len(WAY)
+    sends = [scratch[1 + g * stages : 1 + (g + 1) * stages] for g in range(count)]
+    recvs = [scratch[1 + (count + g) * stages : 1 + (count + g + 1) * stages] for g in range(count)]
+    panel_send, panel_recv, sum_send, sum_recv = scratch[1 + 2 * count * stages :]
     me, mine = lax.axis_index("dp"), lax.axis_index("coef")
     pan = own_ref.shape[1]
 
@@ -82,8 +84,8 @@
         return gram.astype(jnp.bfloat16), three.astype(jnp.bfloat16)
 
     def start(group, stage, values):
-        unit, radix = ORDERS[group][stage]
-        send, recv = (send_a, send_b)[group][stage], (recv_a, recv_b)[group][stage]
+        unit, radix = ORDERS[WAY[group]][stage]
+        send, recv = sends[group][stage], recvs[group][stage]
         chunk = values[0].shape[0] // radix
         copies = []
         for q in range(1, radix):
@@ -118,37 +120,37 @@
             ]
         return values
 
-    def product(left, k):
+    def product(k):
+        left = (left_a, left_b)[WAY[k]]
         right = own_ref[...] if k == 0 else panels[k - 1]
         return jnp.dot(left[...], right, preferred_element_type=jnp.float32)
 
-    blocks = [product(left_a, 0)]
-    for k in GROUPS[0][1:]:
-        fetches[k - 1].wait()
-        blocks.append(product(left_a, k))
-    state_a = start(0, 0, [jnp.concatenate(blocks, axis=1), slope_ref[...]])
-    blocks = []
-    for k in GROUPS[1]:
-        fetches[k - 1].wait()
-        blocks.append(product(left_b, k))
-    state_b = start(1, 0, [jnp.concatenate(blocks, axis=1)])
-    for stage in range(1, len(ORDERS[0])):
-        state_a = start(0, stage, finish(state_a))
-        state_b = start(1, stage, finish(state_b))
-    gram, slope = finish(state_a)
-    band_ref[:, : gram.shape[1]] = gram
-    gradient_ref[...] = slope
-    band_ref[:, gram.shape[1] :] = finish(state_b)[0]
+    state = [None] * count
+    for wave in range(count + stages):
+        for k in range(count):
+            stage = wave - k
+            if stage == 0:
+                if k > 0:
+                    fetches[k - 1].wait()
+                values = [product(k)] + ([slope_ref[...]] if k == 0 else [])
+                state[k] = start(k, 0, values)
+            elif 0 < stage < stages:
+                state[k] = start(k, stage, finish(state[k]))
+            elif stage == stages:
+                values = finish(state[k])
+                band_ref[:, k * pan : (k + 1) * pan] = values[0]
+                if k == 0:
+                    gradient_ref[...] = values[1]
 
 
 def band(own, left_a, left_b, slope):
     dp, coef = lax.axis_size("dp"), lax.axis_size("coef")
     rows, pan = own.shape
-    widths = [len(GROUPS[0]) * pan + LANES, len(GROUPS[1]) * pan]
     buffers = []
-    for order, width in zip(ORDERS, widths):
+    for k, way in enumerate(WAY):
         left = pan
-        for _, radix in order:
+        width = pan + LANES if k == 0 else pan
+        for _, radix in ORDERS[way]:
             left //= radix
             buffers.append(pltpu.VMEM((radix - 1, left, width), jnp.bfloat16))
     each = pan // dp
@@ -167,8 +169,8 @@
         + [
             pltpu.SemaphoreType.DMA((coef // 2,)),
             pltpu.SemaphoreType.DMA((coef // 2,)),
-            pltpu.SemaphoreType.DMA((2, 4, 3)),
-            pltpu.SemaphoreType.DMA((2, 4, 3)),
+            pltpu.SemaphoreType.DMA((len(WAY), 4, 3)),
+            pltpu.SemaphoreType.DMA((len(WAY), 4, 3)),
         ],
         compiler_params=pltpu.CompilerParams(
             collective_id=0, has_side_effects=True, vmem_limit_bytes=48 * 1024 * 1024

time: 85.8 us -> 83.5 us (0.973)
  the two profiles are of different devices: /device:TPU:74 before, /device:TPU:24 now
where the time goes in v3:
time: 83.5 us; the launch traced here: 83.1 us
  Pallas kernels  75.3 us (90%)
  matrix products  4.15 us (5%)
  other arithmetic  1.6 us (2%)
  local copies, waits for them, and re-layouts  1.42 us (2%)
    pallas_call x1, Pallas kernels, band(): pl.pallas_call(functools.partial(band_kernel, dp, coef), out_shape=(jax.S...  75.3 us
    dot_general x2, matrix products, picked(): lax.dot_general(hot.astype(jnp.bfloat16), table, (((1,), (0,)), ((), ()))...  3.06 us

profile of v3, /device:TPU:24, one launch (start us, length us, event | category | flops | bytes accessed | tf_op | source)
XLA Modules:
  0.0 83.1 jit_solution(12784417715454037932)
XLA Ops:
  0.6 0.0 copy-start
  0.6 0.9 %multiply_add_fusion = s32[512]{0:T(512)S(1)} fusion(s32[512]{0:T(512)} %param.8, s32[512]{0:T(512)} %param.7), kind=kLoop, calls=%fused_computation.91 | loop fusion | flops 1024 | bytes 6144 | tf_op jit(solution)/shard_map/add | solution.py:188
  1.5 0.7 fusion.17
  2.3 1.2 %fusion.11 = f32[512,384]{1,0:T(8,128)S(1)} fusion(bf16[128,384]{1,0:T(8,128)(2,1)} %param.13, s32[512]{0:T(512)} %param.9), kind=kOutput, calls=%fused_computation.16 | convolution fusion | flops 50397184 | bytes 886784 | tf_op jit(solution)/shard_map/dot_general | solution.py:19
  3.5 0.0 copy-done
  3.5 1.8 %fusion.4.own_ref = bf16[512,384]{1,0:T(8,128)(2,1)S(1)} fusion(f32[512,384]{1,0:T(8,128)S(1)} %fusion.11, bf16[3072,384]{1,0:T(8,128)(2,1)S(1)} %copy-done, s32[512]{0:T(512)S(1)} %multiply_add_fusion, f32[512]{0:T(512)S(1)} %get-tuple-element.11), kind=kOutput, calls=%fused_computation.5 | convolution fusion | flops 1210122240 | bytes 3543040 | tf_op jit(solution)/shard_map/dot_general | solution.py:19
  5.3 0.4 convolution_convert_fusion.1.left_a
  5.8 0.3 convolution_reduce_fusion
  6.0 0.1 broadcast_in_dim.4.slope_ref
  6.1 0.4 convolution_convert_fusion.left_b
  6.6 75.3 %shard_map.86 = (f32[6,1920]{1,0:T(8,128)S(1)}, f32[6,128]{1,0:T(8,128)S(1)}) custom-call(bf16[512,384]{1,0:T(8,128)(2,1)S(1)} %fusion.4.own_ref, bf16[384,512]{1,0:T(8,128)(2,1)S(1)} %convolution_convert_fusion.1.left_a, bf16[384,512]{1,0:T(8,128)(2,1)S(1)} %convolution_convert_fusion.left_b, f32[384,128]{1,0:T(8,128)S(1)} %broadcast_in_dim.4.slope_ref), custom_call_target="tpu_custom_call" | custom-call | tf_op jit(solution)/shard_map/pallas_call | solution.py:158
  81.8 0.7 copy.10
  82.5 0.6 slice_reduce_fusion
  (2 shorter events, 0.1 us)
Async XLA Ops:
  0.6 2.9 %copy-start = (bf16[3072,384]{1,0:T(8,128)(2,1)S(1)}, bf16[3072,384]{1,0:T(8,128)(2,1)}, u32[]{:S(2)}) copy-start(bf16[3072,384]{1,0:T(8,128)(2,1)} %param.12) | copy-start | bytes 7077892

commit v4 on v3

--- a/solution.py
+++ b/solution.py
@@ -61,18 +61,51 @@
         pl.semaphore_signal(barrier, inc=1, device_id=friend, device_id_type=MESH)
     pl.semaphore_wait(barrier, len(friends))
 
-    fetches = []
-    for k in range(1, coef // 2 + 1):
-        fetch = pltpu.make_async_remote_copy(
-            src_ref=own_ref,
-            dst_ref=panels.at[k - 1],
-            send_sem=panel_send.at[k - 1],
-            recv_sem=panel_recv.at[k - 1],
-            device_id=(me, lax.rem(mine + coef - k, coef)),
+    x = lax.rem(mine, 2)
+    back, beside = (me, lax.rem(mine + coef - 2, coef)), (me, mine + 1 - 2 * x)
+    offsets = [0, 2, 3 - 2 * x, 4, 1 + 2 * x]
+    half = own_ref.shape[0] // 2
+
+    def pass_on(source, slot, part, target):
+        rows = pl.ds(part * half, half)
+        return pltpu.make_async_remote_copy(
+            src_ref=own_ref.at[rows] if source is None else panels.at[source, rows],
+            dst_ref=panels.at[slot, rows],
+            send_sem=panel_send.at[slot, part],
+            recv_sem=panel_recv.at[slot, part],
+            device_id=target,
             device_id_type=MESH,
         )
-        fetch.start()
-        fetches.append(fetch)
+
+    near = [pass_on(None, 0, part, back) for part in range(2)]
+    across = [pass_on(0, 1, part, beside) for part in range(2)]
+    far = [pass_on(0, 2, part, back) for part in range(2)]
+    last_one = [pass_on(None, 3, part, beside) for part in range(2)]
+    last_zero = [pass_on(2, 3, part, beside) for part in range(2)]
+
+    def when_x(value, action):
+        @pl.when(x == value)
+        def _():
+            action()
+
+    for part in range(2):
+        near[part].start()
+    for part in range(2):
+        when_x(1, last_one[part].start)
+
+    def arrive(slot):
+        for part in range(2):
+            if slot == 0:
+                near[part].wait_recv()
+                far[part].start()
+                across[part].start()
+            elif slot == 1:
+                across[part].wait_recv()
+            elif slot == 2:
+                far[part].wait_recv()
+                when_x(0, last_zero[part].start)
+            else:
+                last_one[part].wait_recv()
 
     def packed(gram, slope):
         high = slope.astype(jnp.bfloat16).astype(jnp.float32)
@@ -131,16 +164,25 @@
             stage = wave - k
             if stage == 0:
                 if k > 0:
-                    fetches[k - 1].wait()
+                    arrive(k - 1)
                 values = [product(k)] + ([slope_ref[...]] if k == 0 else [])
                 state[k] = start(k, 0, values)
             elif 0 < stage < stages:
                 state[k] = start(k, stage, finish(state[k]))
             elif stage == stages:
                 values = finish(state[k])
-                band_ref[:, k * pan : (k + 1) * pan] = values[0]
+                column = offsets[k] * pan
+                if k in (2, 4):
+                    column = pl.multiple_of(column, LANES)
+                band_ref[:, pl.ds(column, pan)] = values[0]
                 if k == 0:
                     gradient_ref[...] = values[1]
+    for part in range(2):
+        near[part].wait_send()
+        across[part].wait_send()
+        far[part].wait_send()
+        when_x(1, last_one[part].wait_send)
+        when_x(0, last_zero[part].wait_send)
 
 
 def band(own, left_a, left_b, slope):
@@ -167,8 +209,8 @@
         + buffers
         + buffers
         + [
-            pltpu.SemaphoreType.DMA((coef // 2,)),
-            pltpu.SemaphoreType.DMA((coef // 2,)),
+            pltpu.SemaphoreType.DMA((coef // 2, 2)),
+            pltpu.SemaphoreType.DMA((coef // 2, 2)),
             pltpu.SemaphoreType.DMA((len(WAY), 4, 3)),
             pltpu.SemaphoreType.DMA((len(WAY), 4, 3)),
         ],

time: 83.5 us -> 80.4 us (0.963)
  Pallas kernels: 75.3 us -> 72.4 us
    pallas_call x1, Pallas kernels: 75.3 us -> 72.4 us  [band(): pl.pallas_call(functools.partial(band_kernel, dp, coef), out_shape=(jax.S...]
where the time goes in v4:
time: 80.4 us; the launch traced here: 80.2 us
  Pallas kernels  72.4 us (90%)
  matrix products  4.15 us (5%)
  other arithmetic  1.6 us (2%)
  local copies, waits for them, and re-layouts  1.42 us (2%)
    pallas_call x1, Pallas kernels, band(): pl.pallas_call(functools.partial(band_kernel, dp, coef), out_shape=(jax.S...  72.4 us
    dot_general x2, matrix products, picked(): lax.dot_general(hot.astype(jnp.bfloat16), table, (((1,), (0,)), ((), ()))...  3.06 us

profile of v4, /device:TPU:24, one launch (start us, length us, event | category | flops | bytes accessed | tf_op | source)
XLA Modules:
  0.0 80.2 jit_solution(13123585833896392746)
XLA Ops:
  0.6 0.0 copy-start
  0.6 0.9 %multiply_add_fusion = s32[512]{0:T(512)S(1)} fusion(s32[512]{0:T(512)} %param.8, s32[512]{0:T(512)} %param.7), kind=kLoop, calls=%fused_computation.91 | loop fusion | flops 1024 | bytes 6144 | tf_op jit(solution)/shard_map/add | solution.py:230
  1.5 0.7 fusion.17
  2.3 1.2 %fusion.11 = f32[512,384]{1,0:T(8,128)S(1)} fusion(bf16[128,384]{1,0:T(8,128)(2,1)} %param.13, s32[512]{0:T(512)} %param.9), kind=kOutput, calls=%fused_computation.16 | convolution fusion | flops 50397184 | bytes 886784 | tf_op jit(solution)/shard_map/dot_general | solution.py:19
  3.5 0.0 copy-done
  3.5 1.8 %fusion.4.own_ref = bf16[512,384]{1,0:T(8,128)(2,1)S(1)} fusion(f32[512,384]{1,0:T(8,128)S(1)} %fusion.11, bf16[3072,384]{1,0:T(8,128)(2,1)S(1)} %copy-done, s32[512]{0:T(512)S(1)} %multiply_add_fusion, f32[512]{0:T(512)S(1)} %get-tuple-element.11), kind=kOutput, calls=%fused_computation.5 | convolution fusion | flops 1210122240 | bytes 3543040 | tf_op jit(solution)/shard_map/dot_general | solution.py:19
  5.3 0.4 convolution_convert_fusion.1.left_a
  5.8 0.3 convolution_reduce_fusion
  6.0 0.1 broadcast_in_dim.4.slope_ref
  6.1 0.4 convolution_convert_fusion.left_b
  6.6 72.4 %shard_map.86 = (f32[6,1920]{1,0:T(8,128)S(1)}, f32[6,128]{1,0:T(8,128)S(1)}) custom-call(bf16[512,384]{1,0:T(8,128)(2,1)S(1)} %fusion.4.own_ref, bf16[384,512]{1,0:T(8,128)(2,1)S(1)} %convolution_convert_fusion.1.left_a, bf16[384,512]{1,0:T(8,128)(2,1)S(1)} %convolution_convert_fusion.left_b, f32[384,128]{1,0:T(8,128)S(1)} %broadcast_in_dim.4.slope_ref), custom_call_target="tpu_custom_call" | custom-call | tf_op jit(solution)/shard_map/pallas_call | solution.py:200
  78.9 0.7 copy.10
  79.6 0.6 slice_reduce_fusion
  (2 shorter events, 0.1 us)
Async XLA Ops:
  0.6 2.9 %copy-start = (bf16[3072,384]{1,0:T(8,128)(2,1)S(1)}, bf16[3072,384]{1,0:T(8,128)(2,1)}, u32[]{:S(2)}) copy-start(bf16[3072,384]{1,0:T(8,128)(2,1)} %param.12) | copy-start | bytes 7077892

commit v5 on v4

--- a/solution.py
+++ b/solution.py
@@ -8,7 +8,7 @@
 from jax.experimental.pallas import tpu as pltpu
 from jax.sharding import PartitionSpec as P
 
-ORDERS = (((1, 2), (2, 2), (4, 4), (16, 4)), ((1, 2), (4, 4), (16, 4), (2, 2)))
+ORDERS = (((1, 2), (4, 4), (16, 4), (2, 2)),) * 2
 WAY = (0, 1, 0, 1, 0)
 LANES = 128
 MESH = pl.DeviceIdType.MESH
@@ -160,7 +160,7 @@
 
     state = [None] * count
     for wave in range(count + stages):
-        for k in range(count):
+        for k in reversed(range(count)):
             stage = wave - k
             if stage == 0:
                 if k > 0:

time: 80.4 us -> 76.9 us (0.956); the launches traced: 80.2 us -> 75.8 us
  Pallas kernels: 72.4 us -> 68.4 us
    pallas_call x1, Pallas kernels: 72.4 us -> 68.4 us  [band(): pl.pallas_call(functools.partial(band_kernel, dp, coef), out_shape=(jax.S...]
where the time goes in v5:
time: 76.9 us; the launch traced here: 75.8 us
  Pallas kernels  68.4 us (89%)
  matrix products  3.73 us (5%)
  other arithmetic  1.6 us (2%)
  local copies, waits for them, and re-layouts  1.42 us (2%)
    pallas_call x1, Pallas kernels, band(): pl.pallas_call(functools.partial(band_kernel, dp, coef), out_shape=(jax.S...  68.4 us
    dot_general x2, matrix products, picked(): lax.dot_general(hot.astype(jnp.bfloat16), table, (((1,), (0,)), ((), ()))...  3.06 us

profile of v5, /device:TPU:24, one launch (start us, length us, event | category | flops | bytes accessed | tf_op | source)
XLA Modules:
  0.0 75.8 jit_solution(16286075677332113424)
XLA Ops:
  0.6 0.0 copy-start
  0.6 0.9 %fusion.14 = (bf16[512]{0:T(512)(128)(2,1)S(1)}, f32[512]{0:T(512)S(1)}) fusion(bf16[512]{0:T(512)(128)(2,1)} %param.11, bf16[512]{0:T(512)(128)(2,1)} %param.10), kind=kLoop, calls=%fused_computation.43 | loop fusion | flops 2560 | bytes 5120 | tf_op jit(solution)/shard_map/convert_element_type | solution.py:234
  1.5 1.2 %fusion.8 = f32[512,384]{1,0:T(8,128)S(1)} fusion(bf16[128,384]{1,0:T(8,128)(2,1)} %param.13, s32[512]{0:T(512)} %param.9), kind=kOutput, calls=%fused_computation.12 | convolution fusion | flops 50397184 | bytes 886784 | tf_op jit(solution)/shard_map/dot_general | solution.py:19
  2.7 0.7 multiply_add_fusion
  3.4 0.0 copy-done
  3.4 1.8 %fusion.4.own_ref = bf16[512,384]{1,0:T(8,128)(2,1)S(1)} fusion(f32[512,384]{1,0:T(8,128)S(1)} %fusion.8, bf16[3072,384]{1,0:T(8,128)(2,1)S(1)} %copy-done, s32[512]{0:T(512)S(1)} %multiply_add_fusion, f32[512]{0:T(512)S(1)} %get-tuple-element.11), kind=kOutput, calls=%fused_computation.5 | convolution fusion | flops 1210122240 | bytes 3543040 | tf_op jit(solution)/shard_map/dot_general | solution.py:19
  5.3 0.4 convolution_convert_fusion.left_a.left_b
  5.8 0.3 convolution_reduce_fusion
  6.0 0.1 broadcast_in_dim.4.slope_ref
  6.1 68.4 %shard_map.86 = (f32[6,1920]{1,0:T(8,128)S(1)}, f32[6,128]{1,0:T(8,128)S(1)}) custom-call(bf16[512,384]{1,0:T(8,128)(2,1)S(1)} %fusion.4.own_ref, bf16[384,512]{1,0:T(8,128)(2,1)S(1)} %convolution_convert_fusion.left_a.left_b, bf16[384,512]{1,0:T(8,128)(2,1)S(1)} %convolution_convert_fusion.left_a.left_b, f32[384,128]{1,0:T(8,128)S(1)} %broadcast_in_dim.4.slope_ref), custom_call_target="tpu_custom_call" | custom-call | tf_op jit(solution)/shard_map/pallas_call | solution.py:200
  74.5 0.7 copy.10
  75.2 0.6 slice_reduce_fusion
  (2 shorter events, 0.0 us)
Async XLA Ops:
  0.6 2.8 %copy-start = (bf16[3072,384]{1,0:T(8,128)(2,1)S(1)}, bf16[3072,384]{1,0:T(8,128)(2,1)}, u32[]{:S(2)}) copy-start(bf16[3072,384]{1,0:T(8,128)(2,1)} %param.12) | copy-start | bytes 7077892
